TPU v7x, 256 devices: a whole 4x4x8 slice. The times are simulated.
256 devices in a mesh: seq: 16 (over z, x_lo), wr: 4 (over y), wc: 4 (over x_hi, core).
Axes of the slice: x: 4 (x_hi: 2, x_lo: 2; x = x_hi * 2 + x_lo), y: 4, z: 8, core: 2. Of those that a mesh axis runs over, the one named last changes fastest.
Arguments:
- tokens: bfloat16 [8192, 2048], P('seq', ('wr', 'wc')), may hold values from -6 to 6
- ln_gain: float32 [2, 2048], replicated, may hold values from 0.5 to 1.5
- w_branch: bfloat16 [2, 2048, 4096], P(None, None, ('wr', 'wc')), may hold values from -0.125 to 0.125
- w_outgate: bfloat16 [2, 2048, 4096], P(None, None, ('wr', 'wc')), may hold values from -0.125 to 0.125
- w_gates: bfloat16 [2, 2048, 8], replicated, may hold values from -0.125 to 0.125
- forget_bias: float32 [2, 4], replicated, may hold values from 3.2 to 11
- conv_weight: float32 [2, 4, 4096], P(None, None, ('wr', 'wc')), may hold values from -3 to 3
- conv_bias: float32 [2, 4096], P(None, ('wr', 'wc')), may hold values from -3 to 3
- w_query: float32 [2, 4, 4, 4, 256], P(None, 'wr'), may hold values from -3 to 3
- w_key: float32 [2, 4, 4, 4, 256], P(None, 'wr'), may hold values from -3 to 3
- w_value: float32 [2, 4, 4, 4, 256], P(None, 'wr', None, 'wc'), may hold values from -4 to 4
- skip_gain: float32 [2, 4096], P(None, ('wr', 'wc')), may hold values from 0.5 to 1.5
- norm_gain: float32 [2, 4096], P(None, ('wr', 'wc')), may hold values from 0.5 to 1.5
- w_down: bfloat16 [2, 4096, 2048], P(None, ('wr', 'wc')), may hold values from -0.125 to 0.125
- lengths: int32 [3], replicated, may hold values from 1 to 4096, 8192 in all
- request_prompt: int32 [32], P('seq'), may hold values from 0 to 2
Outputs:
- mixed: bfloat16 [8192, 2048], P('seq', ('wr', 'wc'))
- request_state: bfloat16 [2, 32, 4, 1024, 1024], P(None, 'seq', 'wr', None, 'wc')
- request_conv: bfloat16 [2, 32, 3, 4096], P(None, 'seq', None, ('wr', 'wc'))
Inputs may be any that keep to these rules, and one draw needn't show every extreme that they name: `lengths`: the 3 prompts lie end to end in order and fill all 8192 positions; the longest has exactly 4096 positions.
All inputs are finite; a program needn't handle non-finite values.
Results may differ from a plain program's by a relative error of at most 0.035.
Values may be sent and summed in bfloat16 or wider, within the bound.
A program may use at most 128 MiB of HBM per device.

v0:
```python
import jax
import jax.numpy as jnp
from jax import lax
from jax.sharding import PartitionSpec as P

HEADS = 4
CONV = 4
LAYERS = 2
PROMPTS = 3
EPSILON = 1e-05
GATE_CAP = 15.0
ROW_DIMS = (((0,), (0,)), ((), ()))
FEATURE_DIMS = (((1,), (1,)), ((), ()))


def shifted(value, axis, steps):
    count = lax.axis_size(axis)
    first, last = (max(0, -steps), min(count, count - steps))
    return lax.ppermute(value, axis, [(source, source + steps) for source in range(first, last)])


def span_weights(gathered, lengths, rows, count):
    spans = jnp.arange(count, dtype=jnp.int32)
    seg_end = segment_of(spans * rows + (rows - 1), lengths)
    totals = gathered[:, 0]
    later = jnp.arange(count + 1, dtype=jnp.int32)
    between = (spans[None, None, :] > spans[None, :, None]) & (
        spans[None, None, :] < later[:, None, None]
    )
    logs = jnp.sum(jnp.where(between, totals[None, None, :], 0.0), axis=2)
    seg_in = segment_of(later * rows - 1, lengths)
    keep = (spans[None, :] < later[:, None]) & (seg_end[None, :] == seg_in[:, None])
    state_rows = jnp.where(keep, jnp.exp(logs), 0.0)
    end_rows = []
    for prompt, end_pos in enumerate((lengths[0] - 1, lengths[0] + lengths[1] - 1)):
        holder = end_pos // rows
        pick = (spans == holder).astype(jnp.float32)
        end_cum = jnp.sum(pick * gathered[:, 1 + prompt])
        row = jnp.sum(pick[:, None] * logs[:count], axis=0) + end_cum
        kept = (spans < holder) & (seg_end == prompt)
        kept = kept & (segment_of(holder * rows - 1, lengths) == prompt)
        end_rows.append(jnp.where(kept, jnp.exp(row), 0.0))
    return (state_rows[:count], jnp.stack(end_rows + [state_rows[count]]))


def mix_spans(weights, spans):
    return jnp.sum(weights[:, :, None, None] * spans[None], axis=1)


def norm_rows(source, gain_row):
    widened = source.astype(jnp.float32)
    row_mean = jnp.mean(widened, axis=1, keepdims=True)
    row_var = jnp.mean(widened * widened, axis=1, keepdims=True) - row_mean * row_mean
    return ((widened - row_mean) * lax.rsqrt(row_var + EPSILON) * gain_row).astype(jnp.bfloat16)


def segment_of(positions, lengths):
    bound_one = lengths[0]
    bound_two = lengths[0] + lengths[1]
    return (positions >= bound_one).astype(jnp.int32) + (positions >= bound_two).astype(jnp.int32)


def conv_rows(extended, ext_segment, segment, weight, bias_row):
    row_count = segment.shape[0]
    widened = extended.astype(jnp.float32)
    summed = jnp.zeros((row_count, widened.shape[1]), jnp.float32) + bias_row
    for back_step in range(weight.shape[0]):
        low_row = weight.shape[0] - 1 - back_step
        keep_row = (ext_segment[low_row : low_row + row_count] == segment).astype(jnp.float32)
        summed = (
            summed + weight[back_step] * widened[low_row : low_row + row_count] * keep_row[:, None]
        )
    return jax.nn.silu(summed).astype(jnp.bfloat16)


def block_mix(source, weight):
    row_count = source.shape[0]
    grouped = source.astype(jnp.float32).reshape(row_count, 4, -1)
    mixed = jnp.einsum("tig,ijg->tjg", grouped, weight, precision=lax.Precision.HIGHEST)
    return mixed.reshape(row_count, -1)


def block_terms(queries, key_rows, values, log_forget, in_gate, segment, prev_seg):
    row_count = queries.shape[0]
    cum_log = jnp.cumsum(log_forget)
    row_order = jnp.arange(row_count)
    allowed = (row_order[:, None] >= row_order[None, :]) & (segment[:, None] == segment[None, :])
    exponent = jnp.where(allowed, cum_log[:, None] - cum_log[None, :] + in_gate[None, :], -jnp.inf)
    scores = lax.dot_general(
        queries, key_rows, FEATURE_DIMS, preferred_element_type=jnp.float32
    ) * jnp.exp(exponent)
    in_block = jnp.dot(scores.astype(jnp.bfloat16), values, preferred_element_type=jnp.float32)
    carried = jnp.where(segment == prev_seg, jnp.exp(cum_log), 0.0)
    last_seg = segment[row_count - 1]
    weights = jnp.where(
        segment == last_seg, jnp.exp(cum_log[row_count - 1] - cum_log + in_gate), 0.0
    )
    weighted = (key_rows.astype(jnp.float32) * weights[:, None]).astype(jnp.bfloat16)
    increment = lax.dot_general(weighted, values, ROW_DIMS, preferred_element_type=jnp.float32)
    return (in_block, carried, increment)


def end_part(key_rows, values, cum_log, in_gate, segment, local_end, prompt, holder):
    row_order = jnp.arange(segment.shape[0])
    chosen = holder & (segment == prompt) & (row_order <= local_end)
    weights = jnp.where(chosen, jnp.exp(cum_log[local_end] - cum_log + in_gate), 0.0)
    weighted = (key_rows.astype(jnp.float32) * weights[:, None]).astype(jnp.bfloat16)
    return lax.dot_general(weighted, values, ROW_DIMS, preferred_element_type=jnp.float32)


def body(
    tokens,
    ln_gain,
    w_branch,
    w_outgate,
    w_gates,
    forget_bias,
    conv_weight,
    conv_bias,
    w_query,
    w_key,
    w_value,
    skip_gain,
    norm_gain,
    w_down,
    lengths,
    request_prompt,
):
    tok_rows = tokens.shape[0]
    seq_count = lax.axis_size("seq")
    seq_index = lax.axis_index("seq")
    head_idx = lax.axis_index("wr")
    row_offset = seq_index * tok_rows
    total_rows = tok_rows * seq_count
    row_ids = jnp.arange(tok_rows, dtype=jnp.int32)
    positions = row_offset + row_ids
    segment = segment_of(positions, lengths)
    seg_before = jnp.where(row_offset > 0, segment_of(row_offset - 1, lengths), -1)
    rim_positions = row_offset - (CONV - 1) + jnp.arange(CONV - 1, dtype=jnp.int32)
    rim_segment = jnp.where(rim_positions >= 0, segment_of(rim_positions, lengths), -1)
    ext_segment = jnp.concatenate([rim_segment, segment])
    prompt_starts = [jnp.zeros((), jnp.int32), lengths[0], lengths[0] + lengths[1]]
    prompt_ends = [
        lengths[0] - 1,
        lengths[0] + lengths[1] - 1,
        jnp.zeros((), jnp.int32) + (total_rows - 1),
    ]
    head_mask = (jnp.arange(HEADS, dtype=jnp.int32) == head_idx).astype(jnp.float32)
    current = tokens
    sent_states = []
    sent_edges = []
    for layer_idx in range(LAYERS):
        gathered = lax.all_gather(current, ("wr", "wc"), axis=1, tiled=True)
        normed = norm_rows(gathered, ln_gain[layer_idx])
        branch = jnp.dot(normed, w_branch[layer_idx], preferred_element_type=jnp.float32).astype(
            jnp.bfloat16
        )
        outgate = jnp.dot(normed, w_outgate[layer_idx], preferred_element_type=jnp.float32)
        gate_pre = jnp.dot(normed, w_gates[layer_idx], preferred_element_type=jnp.float32)
        input_pre = jnp.sum(gate_pre[:, :HEADS] * head_mask, axis=1)
        forget_pre = jnp.sum((gate_pre[:, HEADS:] + forget_bias[layer_idx]) * head_mask, axis=1)
        in_gate = GATE_CAP * jnp.tanh(input_pre / GATE_CAP)
        log_forget = jax.nn.log_sigmoid(forget_pre)
        edge_in = shifted(branch[tok_rows - (CONV - 1) :], "seq", 1)
        extended = jnp.concatenate([edge_in, branch], axis=0)
        conv_act = conv_rows(
            extended, ext_segment, segment, conv_weight[layer_idx], conv_bias[layer_idx]
        )
        head_branch, head_act = (
            lax.all_gather(branch, "wc", axis=1, tiled=True),
            lax.all_gather(conv_act, "wc", axis=1, tiled=True),
        )
        head_width = head_act.shape[1]
        queries = block_mix(head_act, w_query[layer_idx, 0]).astype(jnp.bfloat16)
        key_rows = (block_mix(head_act, w_key[layer_idx, 0]) * head_width ** (-0.5)).astype(
            jnp.bfloat16
        )
        values = block_mix(head_branch, w_value[layer_idx, 0]).astype(jnp.bfloat16)
        cum_log = jnp.cumsum(log_forget)
        holders = [
            (end_pos >= row_offset) & (end_pos < row_offset + tok_rows) for end_pos in prompt_ends
        ]
        local_ends = [jnp.clip(end_pos - row_offset, 0, tok_rows - 1) for end_pos in prompt_ends]
        span_logs = lax.all_gather(
            jnp.stack([cum_log[tok_rows - 1], cum_log[local_ends[0]], cum_log[local_ends[1]]]),
            "seq",
        )
        state_rows, end_rows = span_weights(span_logs, lengths, tok_rows, seq_count)
        in_block, carried, increment = block_terms(
            queries, key_rows, values, log_forget, in_gate, segment, seg_before
        )
        parts = [increment] + [
            end_part(
                key_rows,
                values,
                cum_log,
                in_gate,
                segment,
                local_ends[prompt],
                prompt,
                holders[prompt],
            )
            for prompt in range(PROMPTS - 1)
        ]
        slab = head_width // seq_count
        sent = jnp.stack(
            [part.astype(jnp.bfloat16).reshape(seq_count, slab, -1) for part in parts], axis=1
        )
        got = lax.all_to_all(sent, "seq", 0, 0, tiled=True).astype(jnp.float32)
        spans = got[:, 0]
        states = mix_spans(state_rows, spans).astype(jnp.bfloat16)
        state_here = lax.all_to_all(states, "seq", 0, 0, tiled=True).reshape(head_width, -1)
        own_ends = jnp.sum(got[:, 1:], axis=0)
        ends = mix_spans(end_rows, spans) + jnp.concatenate(
            [own_ends, jnp.zeros_like(own_ends[:1])], axis=0
        )
        sent_states.append(lax.all_gather(ends.astype(jnp.bfloat16), "seq", axis=1, tiled=True))
        hidden_parts = in_block + carried[:, None] * jnp.dot(
            queries, state_here, preferred_element_type=jnp.float32
        )
        sums_one, sums_two = lax.psum(
            (jnp.sum(hidden_parts, axis=1), jnp.sum(hidden_parts * hidden_parts, axis=1)), "wc"
        )
        row_mean = sums_one / head_width
        row_var = sums_two / head_width - row_mean * row_mean
        normal_rows = (hidden_parts - row_mean[:, None]) * lax.rsqrt(row_var + EPSILON)[:, None]
        gated = (
            (
                normal_rows * norm_gain[layer_idx]
                + skip_gain[layer_idx] * conv_act.astype(jnp.float32)
            )
            * jax.nn.silu(outgate)
        ).astype(jnp.bfloat16)
        term_rows = jnp.dot(gated, w_down[layer_idx], preferred_element_type=jnp.float32)
        terms = lax.all_to_all(
            term_rows.astype(jnp.bfloat16), ("wr", "wc"), 1, 0, tiled=True
        ).reshape(-1, tok_rows, current.shape[1])
        summed = jnp.sum(terms.astype(jnp.float32), axis=0)
        current = (current.astype(jnp.float32) + summed).astype(jnp.bfloat16)
        for prompt in range(PROMPTS):
            window = lax.dynamic_slice_in_dim(extended, local_ends[prompt] + 1, CONV - 1, 0)
            edge_pos = prompt_ends[prompt] - (CONV - 2) + jnp.arange(CONV - 1, dtype=jnp.int32)
            sent_edges.append(
                jnp.where(
                    ((edge_pos >= prompt_starts[prompt]) & holders[prompt])[:, None],
                    window,
                    jnp.zeros_like(window),
                )
            )
    state_stack = jnp.stack(sent_states)
    edge_stack = lax.psum(jnp.stack(sent_edges), "seq")
    edge_stack = edge_stack.reshape(LAYERS, PROMPTS, edge_stack.shape[1], edge_stack.shape[2])
    chooser = (request_prompt[:, None] == jnp.arange(PROMPTS, dtype=jnp.int32)[None, :]).astype(
        jnp.bfloat16
    )
    request_state = jnp.einsum(
        "rp,lphd->lrhd", chooser, state_stack, preferred_element_type=jnp.float32
    ).astype(jnp.bfloat16)[:, :, None]
    request_conv = jnp.einsum(
        "rp,lpkc->lrkc", chooser, edge_stack, preferred_element_type=jnp.float32
    ).astype(jnp.bfloat16)
    return (current, request_state, request_conv)


def solution(mesh):
    return jax.shard_map(
        body,
        mesh=mesh,
        in_specs=(
            P("seq", ("wr", "wc")),
            P(),
            P(None, None, ("wr", "wc")),
            P(None, None, ("wr", "wc")),
            P(),
            P(),
            P(None, None, ("wr", "wc")),
            P(None, ("wr", "wc")),
            P(None, "wr", None, None, None),
            P(None, "wr", None, None, None),
            P(None, "wr", None, "wc", None),
            P(None, ("wr", "wc")),
            P(None, ("wr", "wc")),
            P(None, ("wr", "wc"), None),
            P(),
            P("seq"),
        ),
        out_specs=(
            P("seq", ("wr", "wc")),
            P(None, "seq", "wr", None, "wc"),
            P(None, "seq", None, ("wr", "wc")),
        ),
        check_vma=False,
    )
```

profile of v0, /device:TPU:16, one launch (start us, length us, event | category | flops | bytes accessed | tf_op | source)
XLA Modules:
  0.0 664.2 jit_solution(5510766327636577990)
XLA Ops:
  14.5 49.2 %all-gather.11.cloned.1.call-done = bf16[512,2048]{1,0:T(8,128)(2,1)} async-done(((bf16[512,128]{1,0:T(8,128)(2,1)}), bf16[512,2048]{1,0:T(8,128)(2,1)}) %all-gather.11.cloned.1.call-update) | async-done | bytes 2097168 | tf_op jit(solution)/shard_map/all_gather | solution.py:153
  63.7 2.4 convert_reduce_fusion.1
  72.5 3.0 collective-permute-start
  83.3 3.7 exponential_select_fusion.7
  86.9 5.6 all-gather.15.cloned.1.call-done
  92.6 1.9 reshape.611
  96.0 21.3 %all-gather.13.cloned.1.call-done = bf16[512,1024]{1,0:T(8,128)(2,1)} async-done(((bf16[512,256]{1,0:T(8,128)(2,1)}), bf16[512,1024]{1,0:T(8,128)(2,1)}) %all-gather.13.cloned.1.call-update) | async-done | bytes 1048592 | tf_op jit(solution)/shard_map/all_gather | solution.py:171
  117.3 1.9 reshape.609
  120.5 3.3 fusion.74
  123.8 1.8 copy.185
  125.6 1.9 fusion.11
  136.0 7.3 %all-to-all-start = ((bf16[16,3,64,256]{3,2,1,0:T(8,128)(2,1)}), bf16[16,3,64,256]{3,2,1,0:T(8,128)(2,1)}, u32[]{:S(2)}, u32[]{:S(2)}) async-start(bf16[16,3,64,256]{3,2,1,0:T(8,128)(2,1)} %pad_maximum_fusion.6), calls=%async_computation | async-start | bytes 3145728 | tf_op jit(solution)/shard_map/all_to_all | solution.py:209
  147.6 2.0 maximum_dynamic-update-slice_fusion
  149.7 56.5 %all-reduce.2 = f32[48]{0:T(128)S(1)} all-reduce(f32[48]{0:T(128)S(1)} %maximum_dynamic-update-slice_fusion), channel_id=2, replica_groups=mesh['seq'=16,'wr'=4,'wc'=4] {'seq'}, use_global_device_ids=true, to_apply=%add.2 | all-reduce | flops 48 | bytes 384
  207.4 1.8 convert_element_type.500
  210.3 3.2 multiply_reduce_fusion.1
  213.4 6.7 %all-to-all-start.1 = ((bf16[16,64,256]{2,1,0:T(8,128)(2,1)}), bf16[16,64,256]{2,1,0:T(8,128)(2,1)}, u32[]{:S(2)}, u32[]{:S(2)}) async-start(bf16[16,64,256]{2,1,0:T(8,128)(2,1)} %multiply_reduce_fusion.1), calls=%async_computation.1 | async-start | bytes 1048576 | tf_op jit(solution)/shard_map/all_to_all | solution.py:212
  221.4 3.2 fusion.21
  226.8 3.5 fusion.28
  230.4 3.3 all-to-all-done.1
  233.7 2.8 fusion.186
  236.5 7.1 %all-reduce.5 = (f32[512]{0:T(512)S(1)}, f32[512]{0:T(512)S(1)}) all-reduce(f32[512]{0:T(512)S(1)} %get-tuple-element.28, f32[512]{0:T(512)S(1)} %get-tuple-element.27), channel_id=1, replica_groups=mesh['seq'=16,'wr'=4,'wc'=4] {'wc'}, use_global_device_ids=true, to_apply=%region_11.12 | all-reduce | flops 1024 | bytes 8192 | tf_op jit(solution)/shard_map/psum | solution.py:221
  243.6 6.0 fusion.17
  249.7 2.1 copy.269
  251.8 32.7 %all_to_all.46 = bf16[512,16,128]{2,0,1:T(8,128)(2,1)S(1)} all-to-all(bf16[512,16,128]{2,0,1:T(8,128)(2,1)S(1)} %bitcast.288), channel_id=1, replica_groups=mesh['seq'=16,'wr'=4,'wc'=4] {'wr','wc'}, dimensions={1} | all-to-all | bytes 4194304 | tf_op jit(solution)/shard_map/all_to_all | solution.py:235
  286.4 46.1 %all-gather.17.cloned.1.call-done = bf16[512,2048]{1,0:T(8,128)(2,1)} async-done(((bf16[512,128]{1,0:T(8,128)(2,1)}), bf16[512,2048]{1,0:T(8,128)(2,1)}) %all-gather.17.cloned.1.call-update) | async-done | bytes 2097168 | tf_op jit(solution)/shard_map/all_gather | solution.py:153
  332.5 2.4 convert_reduce_fusion
  339.2 2.5 collective-permute-start.1
  347.0 2.2 fusion.131
  351.2 2.5 exponential_select_fusion.3
  353.7 8.2 %all-gather.21.cloned.1.call-done = bf16[512,1024]{1,0:T(8,128)(2,1)} async-done(((bf16[512,256]{1,0:T(8,128)(2,1)}), bf16[512,1024]{1,0:T(8,128)(2,1)}) %all-gather.21.cloned.1.call-update) | async-done | bytes 1048592 | tf_op jit(solution)/shard_map/all_gather | solution.py:170
  361.9 2.6 reshape.616
  364.5 3.4 multiply_reduce_fusion.4
  369.0 17.5 %all-gather.19.cloned.1.call-done = bf16[512,1024]{1,0:T(8,128)(2,1)} async-done(((bf16[512,256]{1,0:T(8,128)(2,1)}), bf16[512,1024]{1,0:T(8,128)(2,1)}) %all-gather.19.cloned.1.call-update) | async-done | bytes 1048592 | tf_op jit(solution)/shard_map/all_gather | solution.py:171
  386.4 2.6 reshape.614
  389.1 3.8 copy.199
  392.9 4.5 fusion.71
  397.5 2.9 copy.202
  400.4 3.2 fusion.14
  403.6 2.3 copy.206
  405.8 3.0 fusion.15
  408.8 2.3 copy.207
  411.1 2.5 convolution_convert_fusion.6
  413.6 2.5 convolution_convert_fusion.5
  416.1 2.3 copy.208
  421.6 7.3 %all-to-all-start.3 = ((bf16[16,3,64,256]{3,2,1,0:T(8,128)(2,1)}), bf16[16,3,64,256]{3,2,1,0:T(8,128)(2,1)}, u32[]{:S(2)}, u32[]{:S(2)}) async-start(bf16[16,3,64,256]{3,2,1,0:T(8,128)(2,1)} %pad_maximum_fusion.7), calls=%async_computation.3 | async-start | bytes 3145728 | tf_op jit(solution)/shard_map/all_to_all | solution.py:209
  431.7 2.0 maximum_dynamic-update-slice_fusion.1
  433.7 58.0 %all-reduce.3 = f32[48]{0:T(128)S(1)} all-reduce(f32[48]{0:T(128)S(1)} %maximum_dynamic-update-slice_fusion.1), channel_id=3, replica_groups=mesh['seq'=16,'wr'=4,'wc'=4] {'seq'}, use_global_device_ids=true, to_apply=%add.3 | all-reduce | flops 48 | bytes 384
  499.0 1.8 copy.249
  503.1 1.8 convert_element_type.533
  506.0 3.1 multiply_reduce_fusion
  509.2 6.8 %all-to-all-start.4 = ((bf16[16,64,256]{2,1,0:T(8,128)(2,1)}), bf16[16,64,256]{2,1,0:T(8,128)(2,1)}, u32[]{:S(2)}, u32[]{:S(2)}) async-start(bf16[16,64,256]{2,1,0:T(8,128)(2,1)} %multiply_reduce_fusion), calls=%async_computation.4 | async-start | bytes 1048576 | tf_op jit(solution)/shard_map/all_to_all | solution.py:212
  516.0 3.2 fusion.22
  521.5 3.6 fusion.27
  527.5 4.4 all-to-all-done.4
  531.9 2.2 fusion.185
  534.0 7.2 %all-reduce.4 = (f32[512]{0:T(512)S(1)}, f32[512]{0:T(512)S(1)}) all-reduce(f32[512]{0:T(512)S(1)} %get-tuple-element.26, f32[512]{0:T(512)S(1)} %get-tuple-element.25), channel_id=1, replica_groups=mesh['seq'=16,'wr'=4,'wc'=4] {'wc'}, use_global_device_ids=true, to_apply=%region_24.25 | all-reduce | flops 1024 | bytes 8192 | tf_op jit(solution)/shard_map/psum | solution.py:221
  541.3 5.2 fusion.18
  546.5 3.5 copy.268
  550.0 7.6 %all-to-all-start.5 = ((bf16[512,16,128]{2,0,1:T(8,128)(2,1)}), bf16[512,16,128]{2,0,1:T(8,128)(2,1)S(1)}, u32[]{:S(2)}, u32[]{:S(2)}) async-start(bf16[512,16,128]{2,0,1:T(8,128)(2,1)} %bitcast.287), calls=%async_computation.5 | async-start | bytes 4194304 | tf_op jit(solution)/shard_map/all_to_all | solution.py:235
  559.4 84.2 %psum.39 = bf16[2,3,3,256]{3,1,2,0:T(4,128)(2,1)S(1)} all-reduce(bf16[2,3,3,256]{3,1,2,0:T(4,128)(2,1)S(1)} %copy.221), channel_id=1, replica_groups=mesh['seq'=16,'wr'=4,'wc'=4] {'seq'}, use_global_device_ids=true, to_apply=%region_38.39 | all-reduce | flops 4608 | bytes 18432 | tf_op jit(solution)/shard_map/psum | solution.py:251
  644.5 4.1 copy.271
  650.1 2.8 copy.270
  652.9 2.6 fusion.10
  (290 shorter events, 78.6 us)
Async XLA Ops:
  7.2 56.5 %all-gather.11.cloned.1.call-start = ((), (), s32[]{:S(2)}) async-start(), calls=%async_computation.6 | async-start | bytes 2228224 | tf_op jit(solution)/shard_map/all_gather | solution.py:153
  7.9 84.7 %all-gather.15.cloned.1.call-start = ((), (), s32[]{:S(2)}) async-start(), calls=%async_computation.8 | async-start | bytes 1310720 | tf_op jit(solution)/shard_map/all_gather | solution.py:170
  12.5 63.7 %copy-start.36 = (s32[512]{0:T(512)}, s32[512]{0:T(512)S(1)}, u32[]{:S(2)}) copy-start(s32[512]{0:T(512)S(1)} %convert_add_fusion) | copy-start | bytes 6148
  67.8 12.2 %copy-start.5 = (bf16[512,2048]{1,0:T(8,128)(2,1)}, bf16[512,2048]{1,0:T(8,128)(2,1)S(1)}, u32[]{:S(2)}) copy-start(bf16[512,2048]{1,0:T(8,128)(2,1)S(1)} %fusion.2) | copy-start | bytes 6291460
  69.2 10.8 %copy-start.22 = (bf16[2,2048,8]{1,2,0:T(8,128)(2,1)S(1)}, bf16[2,2048,8]{1,2,0:T(8,128)(2,1)}, u32[]{:S(2)}) copy-start(bf16[2,2048,8]{1,2,0:T(8,128)(2,1)} %param.20) | copy-start | bytes 196612
  69.2 48.1 %all-gather.13.cloned.1.call-start = ((), (), s32[]{:S(2)}) async-start(), calls=%async_computation.7 | async-start | bytes 1310720 | tf_op jit(solution)/shard_map/all_gather | solution.py:171
  70.6 10.0 %copy-start.25 = (f32[512]{0:T(512)}, f32[512]{0:T(512)S(1)}, u32[]{:S(2)}) copy-start(f32[512]{0:T(512)S(1)} %get-tuple-element.95) | copy-start | bytes 6148
  70.6 10.0 %copy-start.27 = (f32[512]{0:T(512)}, f32[512]{0:T(512)S(1)}, u32[]{:S(2)}) copy-start(f32[512]{0:T(512)S(1)} %get-tuple-element.96) | copy-start | bytes 6148
  70.6 10.0 %copy-start.29 = (f32[512]{0:T(512)}, f32[512]{0:T(512)S(1)}, u32[]{:S(2)}) copy-start(f32[512]{0:T(512)S(1)} %get-tuple-element.97) | copy-start | bytes 6148
  72.5 5.3 collective-permute-start
  80.0 14.5 %copy-start.54 = (f32[4]{0:T(128)}, f32[4]{0:T(128)S(1)}, u32[]{:S(2)}) copy-start(f32[4]{0:T(128)S(1)} %compare_convert_fusion.6) | copy-start | bytes 52
  120.5 5.1 copy-start
  136.0 7.3 %copy-start.24 = (f32[2,1,4,4,256]{4,3,2,1,0:T(4,128)S(1)}, f32[2,1,4,4,256]{4,3,2,1,0:T(4,128)}, u32[]{:S(2)}) copy-start(f32[2,1,4,4,256]{4,3,2,1,0:T(4,128)} %param.24) | copy-start | bytes 98308
  136.0 9.0 %copy-start.71 = (u32[256]{0:T(256)S(1)}, u32[256]{0:T(256)}, u32[]{:S(2)}) copy-start(u32[256]{0:T(256)} %constant.135) | copy-start | bytes 3076
  136.0 71.3 %all-to-all-start = ((bf16[16,3,64,256]{3,2,1,0:T(8,128)(2,1)}), bf16[16,3,64,256]{3,2,1,0:T(8,128)(2,1)}, u32[]{:S(2)}, u32[]{:S(2)}) async-start(bf16[16,3,64,256]{3,2,1,0:T(8,128)(2,1)} %pad_maximum_fusion.6), calls=%async_computation | async-start | bytes 3145728 | tf_op jit(solution)/shard_map/all_to_all | solution.py:209
  146.9 60.4 %copy-start.50 = (s32[17]{0:T(128)}, s32[17]{0:T(128)S(1)}, u32[]{:S(2)}) copy-start(s32[17]{0:T(128)S(1)} %fusion.170) | copy-start | bytes 208
  147.6 59.7 %copy-start.52 = (s32[16]{0:T(128)}, s32[16]{0:T(128)S(1)}, u32[]{:S(2)}) copy-start(s32[16]{0:T(128)S(1)} %fusion.169) | copy-start | bytes 196
  147.6 59.5 %copy-start.31 = (pred[17,16]{0,1:T(8,128)(4,1)}, pred[17,16]{0,1:T(8,128)(4,1)S(1)}, u32[]{:S(2)}) copy-start(pred[17,16]{0,1:T(8,128)(4,1)S(1)} %iota_compare_fusion.2) | copy-start | bytes 820
  147.6 59.5 %copy-start.32 = (pred[16,16]{1,0:T(8,128)(4,1)}, pred[16,16]{1,0:T(8,128)(4,1)S(1)}, u32[]{:S(2)}) copy-start(pred[16,16]{1,0:T(8,128)(4,1)S(1)} %iota_compare_fusion.1) | copy-start | bytes 772
  209.2 11.1 %copy-start.60 = (f32[2,256]{1,0:T(2,128)S(1)}, f32[2,256]{1,0:T(2,128)}, u32[]{:S(2)}) copy-start(f32[2,256]{1,0:T(2,128)} %param.27) | copy-start | bytes 6148
  209.2 11.7 %copy-start.61 = (f32[2,256]{1,0:T(2,128)S(1)}, f32[2,256]{1,0:T(2,128)}, u32[]{:S(2)}) copy-start(f32[2,256]{1,0:T(2,128)} %param.28) | copy-start | bytes 6148
  213.4 20.2 %all-to-all-start.1 = ((bf16[16,64,256]{2,1,0:T(8,128)(2,1)}), bf16[16,64,256]{2,1,0:T(8,128)(2,1)}, u32[]{:S(2)}, u32[]{:S(2)}) async-start(bf16[16,64,256]{2,1,0:T(8,128)(2,1)} %multiply_reduce_fusion.1), calls=%async_computation.1 | async-start | bytes 1048576 | tf_op jit(solution)/shard_map/all_to_all | solution.py:212
  220.2 112.3 %all-gather.17.cloned.1.call-start = ((), (), s32[]{:S(2)}) async-start(), calls=%async_computation.9 | async-start | bytes 2228224 | tf_op jit(solution)/shard_map/all_gather | solution.py:153
  221.4 5.4 copy-start.37
  221.4 5.4 copy-start.49
  226.8 6.9 %copy-start.65 = (f32[512]{0:T(512)S(1)}, f32[512]{0:T(512)}, u32[]{:S(2)}) copy-start(f32[512]{0:T(512)} %get-tuple-element.57) | copy-start | bytes 6148
  230.4 13.3 %copy-start.20 = (bf16[512,256]{1,0:T(8,128)(2,1)S(1)}, bf16[512,256]{1,0:T(8,128)(2,1)}, u32[]{:S(2)}) copy-start(bf16[512,256]{1,0:T(8,128)(2,1)} %multiply_convert_fusion.5) | copy-start | bytes 786436
  286.1 75.8 %all-gather.21.cloned.1.call-start = ((), (), s32[]{:S(2)}) async-start(), calls=%async_computation.11 | async-start | bytes 1310720 | tf_op jit(solution)/shard_map/all_gather | solution.py:170
  337.0 7.0 %copy-start.26 = (f32[512]{0:T(512)S(1)}, f32[512]{0:T(512)}, u32[]{:S(2)}) copy-start(f32[512]{0:T(512)} %copy-done.25) | copy-start | bytes 6148
  337.0 7.0 %copy-start.28 = (f32[512]{0:T(512)S(1)}, f32[512]{0:T(512)}, u32[]{:S(2)}) copy-start(f32[512]{0:T(512)} %copy-done.27) | copy-start | bytes 6148
  337.0 7.0 %copy-start.30 = (f32[512]{0:T(512)S(1)}, f32[512]{0:T(512)}, u32[]{:S(2)}) copy-start(f32[512]{0:T(512)} %copy-done.29) | copy-start | bytes 6148
  337.0 7.0 %copy-start.41 = (f32[1,1,256]{2,1,0:T(1,128)S(1)}, f32[1,1,256]{2,1,0:T(1,128)}, u32[]{:S(2)}) copy-start(f32[1,1,256]{2,1,0:T(1,128)} %get-tuple-element.80) | copy-start | bytes 3076
  337.0 7.0 %copy-start.42 = (f32[1,1,256]{2,1,0:T(1,128)S(1)}, f32[1,1,256]{2,1,0:T(1,128)}, u32[]{:S(2)}) copy-start(f32[1,1,256]{2,1,0:T(1,128)} %get-tuple-element.81) | copy-start | bytes 3076
  337.0 7.0 %copy-start.43 = (f32[1,1,256]{2,1,0:T(1,128)S(1)}, f32[1,1,256]{2,1,0:T(1,128)}, u32[]{:S(2)}) copy-start(f32[1,1,256]{2,1,0:T(1,128)} %get-tuple-element.86) | copy-start | bytes 3076
  337.1 7.0 %copy-start.44 = (f32[1,1,256]{2,1,0:T(1,128)S(1)}, f32[1,1,256]{2,1,0:T(1,128)}, u32[]{:S(2)}) copy-start(f32[1,1,256]{2,1,0:T(1,128)} %get-tuple-element.87) | copy-start | bytes 3076
  337.1 7.0 %copy-start.45 = (f32[1,256]{1,0:T(1,128)S(1)}, f32[1,256]{1,0:T(1,128)}, u32[]{:S(2)}) copy-start(f32[1,256]{1,0:T(1,128)} %get-tuple-element.108) | copy-start | bytes 3076
  338.5 7.5 %copy-start.33 = (f32[1,1,4,1,256]{4,3,2,1,0:T(1,128)S(1)}, f32[1,1,4,1,256]{4,3,2,1,0:T(1,128)}, u32[]{:S(2)}) copy-start(f32[1,1,4,1,256]{4,3,2,1,0:T(1,128)} %get-tuple-element.78) | copy-start | bytes 12292
  338.5 47.9 %all-gather.19.cloned.1.call-start = ((), (), s32[]{:S(2)}) async-start(), calls=%async_computation.10 | async-start | bytes 1310720 | tf_op jit(solution)/shard_map/all_gather | solution.py:171
  339.2 3.8 collective-permute-start.1
  345.2 4.7 copy-start.46
  345.2 6.0 copy-start.56
  345.2 6.0 copy-start.57
  345.2 6.0 copy-start.58
  350.6 38.5 %copy-start.34 = (f32[512]{0:T(512)}, f32[512]{0:T(512)S(1)}, u32[]{:S(2)}) copy-start(f32[512]{0:T(512)S(1)} %get-tuple-element.54) | copy-start | bytes 6148
  421.6 9.3 %copy-start.63 = (f32[16]{0:T(128)S(1)}, f32[16]{0:T(128)}, u32[]{:S(2)}) copy-start(f32[16]{0:T(128)} %get-tuple-element.33) | copy-start | bytes 196
  421.6 9.3 %copy-start.64 = (f32[16]{0:T(128)S(1)}, f32[16]{0:T(128)}, u32[]{:S(2)}) copy-start(f32[16]{0:T(128)} %get-tuple-element.34) | copy-start | bytes 196
  421.6 81.6 %all-to-all-start.3 = ((bf16[16,3,64,256]{3,2,1,0:T(8,128)(2,1)}), bf16[16,3,64,256]{3,2,1,0:T(8,128)(2,1)}, u32[]{:S(2)}, u32[]{:S(2)}) async-start(bf16[16,3,64,256]{3,2,1,0:T(8,128)(2,1)} %pad_maximum_fusion.7), calls=%async_computation.3 | async-start | bytes 3145728 | tf_op jit(solution)/shard_map/all_to_all | solution.py:209
  428.9 215.6 %all-gather.23.cloned.1.call-start = ((), (), s32[]{:S(2)}) async-start(), calls=%async_computation.12 | async-start | bytes 1671168 | tf_op jit(solution)/shard_map/all_gather | solution.py:217
  431.7 69.2 %copy-start.51 = (s32[17]{0:T(128)S(1)}, s32[17]{0:T(128)}, u32[]{:S(2)}) copy-start(s32[17]{0:T(128)} %copy-done.50) | copy-start | bytes 208
  431.7 69.2 %copy-start.53 = (s32[16]{0:T(128)S(1)}, s32[16]{0:T(128)}, u32[]{:S(2)}) copy-start(s32[16]{0:T(128)} %copy-done.52) | copy-start | bytes 196
  509.2 22.7 %all-to-all-start.4 = ((bf16[16,64,256]{2,1,0:T(8,128)(2,1)}), bf16[16,64,256]{2,1,0:T(8,128)(2,1)}, u32[]{:S(2)}, u32[]{:S(2)}) async-start(bf16[16,64,256]{2,1,0:T(8,128)(2,1)} %multiply_reduce_fusion), calls=%async_computation.4 | async-start | bytes 1048576 | tf_op jit(solution)/shard_map/all_to_all | solution.py:212
  515.9 5.5 copy-start.35
  516.0 5.5 copy-start.38
  516.0 5.5 copy-start.48
  516.0 134.2 %all-gather.25.cloned.1.call-start = ((), (), s32[]{:S(2)}) async-start(), calls=%async_computation.13 | async-start | bytes 1671168 | tf_op jit(solution)/shard_map/all_gather | solution.py:217
  525.0 6.8 %copy-start.47 = (f32[512]{0:T(512)S(1)}, f32[512]{0:T(512)}, u32[]{:S(2)}) copy-start(f32[512]{0:T(512)} %get-tuple-element.53) | copy-start | bytes 6148
  526.8 14.5 %copy-start.4 = (bf16[512,2048]{1,0:T(8,128)(2,1)S(1)}, bf16[512,2048]{1,0:T(8,128)(2,1)}, u32[]{:S(2)}) copy-start(bf16[512,2048]{1,0:T(8,128)(2,1)} %copy-done.3) | copy-start | bytes 6291460
  526.8 14.5 %copy-start.19 = (bf16[512,256]{1,0:T(8,128)(2,1)S(1)}, bf16[512,256]{1,0:T(8,128)(2,1)}, u32[]{:S(2)}) copy-start(bf16[512,256]{1,0:T(8,128)(2,1)} %multiply_convert_fusion.3) | copy-start | bytes 786436
  526.8 14.5 %copy-start.66 = (f32[1,256]{1,0:T(1,128)S(1)}, f32[1,256]{1,0:T(1,128)}, u32[]{:S(2)}) copy-start(f32[1,256]{1,0:T(1,128)} %get-tuple-element.102) | copy-start | bytes 3076
  526.8 14.5 %copy-start.67 = (f32[1,256]{1,0:T(1,128)S(1)}, f32[1,256]{1,0:T(1,128)}, u32[]{:S(2)}) copy-start(f32[1,256]{1,0:T(1,128)} %get-tuple-element.100) | copy-start | bytes 3076
  550.0 9.0 %copy-start.8 = (bf16[512,256]{1,0:T(8,128)(2,1)S(1)}, bf16[512,256]{1,0:T(8,128)(2,1)}, u32[]{:S(2)}) copy-start(bf16[512,256]{1,0:T(8,128)(2,1)} %convolution_convert_fusion.11) | copy-start | bytes 786436
  550.0 9.2 %copy-start.9 = (bf16[512,256]{1,0:T(8,128)(2,1)S(1)}, bf16[512,256]{1,0:T(8,128)(2,1)}, u32[]{:S(2)}) copy-start(bf16[512,256]{1,0:T(8,128)(2,1)} %convolution_convert_fusion.10) | copy-start | bytes 786436
  550.0 93.7 %copy-start.70 = (s32[2]{0:T(128)S(1)}, s32[2]{0:T(128)}, u32[]{:S(2)}) copy-start(s32[2]{0:T(128)} %param.31) | copy-start | bytes 28
  550.0 98.6 %all-to-all-start.5 = ((bf16[512,16,128]{2,0,1:T(8,128)(2,1)}), bf16[512,16,128]{2,0,1:T(8,128)(2,1)S(1)}, u32[]{:S(2)}, u32[]{:S(2)}) async-start(bf16[512,16,128]{2,0,1:T(8,128)(2,1)} %bitcast.287), calls=%async_computation.5 | async-start | bytes 4194304 | tf_op jit(solution)/shard_map/all_to_all | solution.py:235
  (23 other events, 46.9 us)
Sparse Core Ops, SparseCore 0:
  10.6 53.0 all-gather.10
  69.3 23.1 all-gather.14
  94.4 22.8 all-gather.12
  286.2 46.2 all-gather.16
  338.6 23.1 all-gather.20
  363.5 22.8 all-gather.18
  499.2 73.1 all-gather.22
  574.1 70.0 all-gather.24
where the time goes:
time: 669 us; the launch traced here: 664 us
  blocking collectives  246 us (37%)
  waiting for transfers between devices  158 us (24%)
  local copies, waits for them, and re-layouts  72 us (11%)
  other arithmetic  69.9 us (10%)
  matrix products  56.6 us (8%)
  starting transfers between devices  41.7 us (6%)
  between operations  20.6 us (3%)
    unnamed x2, blocking collectives  114 us
    all_gather x2, waiting for transfers between devices, body(): gathered = lax.all_gather(current, ('wr', 'wc'), axis=1, tiled=True)  95.3 us
    psum x1, blocking collectives, body(): edge_stack = lax.psum(jnp.stack(sent_edges), 'seq')  84.2 us
    all_gather x2, waiting for transfers between devices, body(): lax.all_gather(conv_act, 'wc', axis=1, tiled=True)  38.8 us
    all_to_all x1, blocking collectives, body(): lax.all_to_all(term_rows.astype(jnp.bfloat16), ('wr', 'wc'), 1, 0, tiled=...  32.7 us
    unnamed x154, local copies, waits for them, and re-layouts  15 us
    all_to_all x2, starting transfers between devices, body(): got = lax.all_to_all(sent, 'seq', 0, 0, tiled=True).astype(jnp.float32)  14.6 us
    psum x2, blocking collectives, body(): lax.psum((jnp.sum(hidden_parts, axis=1), jnp.sum(hidden_parts * hidden_pa...  14.3 us
  transfers between devices with their start and end apart: 15, of which 9 were waited for; matrix products, arithmetic and copies ran while one was open for 16% of the time, Pallas kernels for 0%

commit v1 on v0

--- a/solution.py
+++ b/solution.py
@@ -168,7 +168,9 @@
         )
         head_branch, head_act = (
             lax.all_gather(branch, "wc", axis=1, tiled=True),
-            lax.all_gather(conv_act, "wc", axis=1, tiled=True),
+            jnp.concatenate(
+                lax.all_to_all(jnp.stack([conv_act] * lax.axis_size("wc")), "wc", 0, 0), axis=1
+            ),
         )
         head_width = head_act.shape[1]
         queries = block_mix(head_act, w_query[layer_idx, 0]).astype(jnp.bfloat16)

time: 669 us -> 650 us (0.972); the launches traced: 664 us -> 638 us
  waiting for transfers between devices: 158 us -> 125 us
  starting transfers between devices: 41.7 us -> 50.2 us
    all_gather x2 -> x0, waiting for transfers between devices: 38.8 us -> none  [body(): lax.all_gather(conv_act, 'wc', axis=1, tiled=True)]
    all_to_all x0 -> x2, waiting for transfers between devices: none -> 29.1 us  [body(): lax.all_to_all(jnp.stack([conv_act] * lax.axis_size('wc')), 'wc', 0, 0)]
    all_gather x2, waiting for transfers between devices: 13.8 us -> 0.01 us  [body(): lax.all_gather(branch, 'wc', axis=1, tiled=True)]
    all_gather x2, waiting for transfers between devices: 95.3 us -> 86 us  [body(): gathered = lax.all_gather(current, ('wr', 'wc'), axis=1, tiled=True)]
    reshape x6 -> x2, local copies, waits for them, and re-layouts: 14.2 us -> 5.33 us  [block_mix(): grouped = source.astype(jnp.float32).reshape(row_count, 4, -1)]
    all_to_all x0 -> x2, starting transfers between devices: none -> 7.79 us  [body(): lax.all_to_all(jnp.stack([conv_act] * lax.axis_size('wc')), 'wc', 0, 0)]
    unnamed x154 -> x148, local copies, waits for them, and re-layouts: 15 us -> 15.5 us
  transfers between devices with their start and end apart: 15 -> 15, of which waited for: 9 -> 8; matrix products, arithmetic and copies ran while one was open for 16% -> 21% of each run, Pallas kernels for 0% -> 0%
where the time goes in v1:
time: 650 us; the launch traced here: 638 us
  blocking collectives  243 us (37%)
  waiting for transfers between devices  125 us (19%)
  local copies, waits for them, and re-layouts  75.4 us (12%)
  other arithmetic  71.6 us (11%)
  matrix products  52 us (8%)
  starting transfers between devices  50.2 us (8%)
  between operations  20.9 us (3%)
    unnamed x2, blocking collectives  112 us
    all_gather x2, waiting for transfers between devices, body(): gathered = lax.all_gather(current, ('wr', 'wc'), axis=1, tiled=True)  86 us
    psum x1, blocking collectives, body(): edge_stack = lax.psum(jnp.stack(sent_edges), 'seq')  83.6 us
    all_to_all x1, blocking collectives, body(): lax.all_to_all(term_rows.astype(jnp.bfloat16), ('wr', 'wc'), 1, 0, tiled=...  32.2 us
    all_to_all x2, waiting for transfers between devices, body(): lax.all_to_all(jnp.stack([conv_act] * lax.axis_size('wc')), 'wc', 0, 0)  29.1 us
    all_to_all x2, starting transfers between devices, body(): got = lax.all_to_all(sent, 'seq', 0, 0, tiled=True).astype(jnp.float32)  17.4 us
    dot_general x4, matrix products, block_mix(): jnp.einsum('tig,ijg->tjg', grouped, weight, precision=lax.Precision.HIGHEST)  15.5 us
    unnamed x148, local copies, waits for them, and re-layouts  15.5 us
  transfers between devices with their start and end apart: 15, of which 8 were waited for; matrix products, arithmetic and copies ran while one was open for 21% of the time, Pallas kernels for 0%

profile of v1, /device:TPU:16, one launch (start us, length us, event | category | flops | bytes accessed | tf_op | source)
XLA Modules:
  0.0 638.1 jit_solution(16768068108584327377)
XLA Ops:
  22.4 41.3 %all-gather.9.cloned.1.call-done = bf16[512,2048]{1,0:T(8,128)(2,1)} async-done(((bf16[512,128]{1,0:T(8,128)(2,1)}), bf16[512,2048]{1,0:T(8,128)(2,1)}) %all-gather.9.cloned.1.call-update) | async-done | bytes 2097168 | tf_op jit(solution)/shard_map/all_gather | solution.py:153
  63.7 2.4 convert_reduce_fusion.1
  70.6 2.5 collective-permute-start
  76.1 3.5 all-to-all-start
  82.2 3.8 exponential_select_fusion.7
  86.0 15.1 %all-to-all-done = bf16[4,512,256]{1,2,0:T(8,128)(2,1)S(1)} async-done(((bf16[4,512,256]{1,2,0:T(8,128)(2,1)}), bf16[4,512,256]{1,2,0:T(8,128)(2,1)S(1)}, u32[]{:S(2)}, u32[]{:S(2)}) %all-to-all-start) | async-done | bytes 1048608 | tf_op jit(solution)/shard_map/all_to_all | solution.py:172
  101.1 3.6 fusion.60
  104.7 1.9 copy.188
  106.6 2.9 fusion.11
  109.4 1.8 copy.192
  114.5 2.3 copy.194
  116.8 2.7 reshape.616
  119.5 2.6 multiply_reduce_fusion.5
  125.4 8.5 %all-to-all-start.1 = ((bf16[16,3,64,256]{3,2,1,0:T(8,128)(2,1)}), bf16[16,3,64,256]{3,2,1,0:T(8,128)(2,1)}, u32[]{:S(2)}, u32[]{:S(2)}) async-start(bf16[16,3,64,256]{3,2,1,0:T(8,128)(2,1)} %pad_maximum_fusion.6), calls=%async_computation.1 | async-start | bytes 3145728 | tf_op jit(solution)/shard_map/all_to_all | solution.py:211
  138.3 2.1 maximum_dynamic-update-slice_fusion
  140.4 55.9 %all-reduce.2 = f32[48]{0:T(128)S(1)} all-reduce(f32[48]{0:T(128)S(1)} %maximum_dynamic-update-slice_fusion), channel_id=2, replica_groups=mesh['seq'=16,'wr'=4,'wc'=4] {'seq'}, use_global_device_ids=true, to_apply=%add.2 | all-reduce | flops 48 | bytes 384
  200.5 3.2 multiply_reduce_fusion.1
  203.6 6.9 %all-to-all-start.2 = ((bf16[16,64,256]{2,1,0:T(8,128)(2,1)}), bf16[16,64,256]{2,1,0:T(8,128)(2,1)}, u32[]{:S(2)}, u32[]{:S(2)}) async-start(bf16[16,64,256]{2,1,0:T(8,128)(2,1)} %multiply_reduce_fusion.1), calls=%async_computation.2 | async-start | bytes 1048576 | tf_op jit(solution)/shard_map/all_to_all | solution.py:214
  211.7 3.6 fusion.21
  217.4 3.6 fusion.28
  221.0 3.0 all-to-all-done.2
  224.0 2.8 fusion.190
  226.8 7.1 %all-reduce.5 = (f32[512]{0:T(512)S(1)}, f32[512]{0:T(512)S(1)}) all-reduce(f32[512]{0:T(512)S(1)} %get-tuple-element.28, f32[512]{0:T(512)S(1)} %get-tuple-element.27), channel_id=1, replica_groups=mesh['seq'=16,'wr'=4,'wc'=4] {'wc'}, use_global_device_ids=true, to_apply=%region_11.12 | all-reduce | flops 1024 | bytes 8192 | tf_op jit(solution)/shard_map/psum | solution.py:223
  233.9 6.1 fusion.17
  240.0 2.1 copy.281
  242.2 32.2 %all_to_all.56 = bf16[512,16,128]{2,0,1:T(8,128)(2,1)S(1)} all-to-all(bf16[512,16,128]{2,0,1:T(8,128)(2,1)S(1)} %bitcast.284), channel_id=1, replica_groups=mesh['seq'=16,'wr'=4,'wc'=4] {'wr','wc'}, dimensions={1} | all-to-all | bytes 4194304 | tf_op jit(solution)/shard_map/all_to_all | solution.py:237
  278.0 44.7 %all-gather.13.cloned.1.call-done = bf16[512,2048]{1,0:T(8,128)(2,1)} async-done(((bf16[512,128]{1,0:T(8,128)(2,1)}), bf16[512,2048]{1,0:T(8,128)(2,1)}) %all-gather.13.cloned.1.call-update) | async-done | bytes 2097168 | tf_op jit(solution)/shard_map/all_gather | solution.py:153
  322.7 2.4 convert_reduce_fusion
  330.5 2.5 collective-permute-start.1
  336.4 1.8 copy.201
  338.2 2.0 stack.69
  340.3 4.3 all-to-all-start.4
  346.4 2.4 exponential_select_fusion.3
  348.8 14.0 %all-to-all-done.4 = bf16[4,512,256]{1,2,0:T(8,128)(2,1)} async-done(((bf16[4,512,256]{1,2,0:T(8,128)(2,1)}), bf16[4,512,256]{1,2,0:T(8,128)(2,1)}, u32[]{:S(2)}, u32[]{:S(2)}) %all-to-all-start.4) | async-done | bytes 1048608 | tf_op jit(solution)/shard_map/all_to_all | solution.py:172
  362.8 4.9 fusion.57
  367.7 2.9 copy.206
  370.7 3.2 fusion.14
  373.9 2.3 copy.210
  376.2 2.9 fusion.15
  379.1 2.3 copy.211
  381.4 2.3 copy.212
  383.7 2.7 reshape.620
  386.3 3.3 multiply_reduce_fusion.4
  389.7 1.8 copy.242
  391.5 1.8 convolution_convert_fusion.6
  396.9 8.8 %all-to-all-start.5 = ((bf16[16,3,64,256]{3,2,1,0:T(8,128)(2,1)}), bf16[16,3,64,256]{3,2,1,0:T(8,128)(2,1)}, u32[]{:S(2)}, u32[]{:S(2)}) async-start(bf16[16,3,64,256]{3,2,1,0:T(8,128)(2,1)} %pad_maximum_fusion.7), calls=%async_computation.5 | async-start | bytes 3145728 | tf_op jit(solution)/shard_map/all_to_all | solution.py:211
  409.7 2.0 maximum_dynamic-update-slice_fusion.1
  411.7 56.2 %all-reduce.3 = f32[48]{0:T(128)S(1)} all-reduce(f32[48]{0:T(128)S(1)} %maximum_dynamic-update-slice_fusion.1), channel_id=3, replica_groups=mesh['seq'=16,'wr'=4,'wc'=4] {'seq'}, use_global_device_ids=true, to_apply=%add.3 | all-reduce | flops 48 | bytes 384
  469.9 2.0 bitcast_select_fusion.2
  474.7 1.8 copy.253
  481.7 3.1 multiply_reduce_fusion
  484.8 6.7 %all-to-all-start.6 = ((bf16[16,64,256]{2,1,0:T(8,128)(2,1)}), bf16[16,64,256]{2,1,0:T(8,128)(2,1)}, u32[]{:S(2)}, u32[]{:S(2)}) async-start(bf16[16,64,256]{2,1,0:T(8,128)(2,1)} %multiply_reduce_fusion), calls=%async_computation.6 | async-start | bytes 1048576 | tf_op jit(solution)/shard_map/all_to_all | solution.py:214
  491.6 3.5 fusion.22
  497.3 3.6 fusion.27
  503.4 4.0 all-to-all-done.6
  507.4 2.2 fusion.189
  509.6 7.6 %all-reduce.4 = (f32[512]{0:T(512)S(1)}, f32[512]{0:T(512)S(1)}) all-reduce(f32[512]{0:T(512)S(1)} %get-tuple-element.26, f32[512]{0:T(512)S(1)} %get-tuple-element.25), channel_id=1, replica_groups=mesh['seq'=16,'wr'=4,'wc'=4] {'wc'}, use_global_device_ids=true, to_apply=%region_24.25 | all-reduce | flops 1024 | bytes 8192 | tf_op jit(solution)/shard_map/psum | solution.py:223
  517.3 5.2 fusion.18
  522.5 3.5 copy.280
  526.0 6.0 all-to-all-start.7
  533.9 83.6 %psum.39 = bf16[2,3,3,256]{3,1,2,0:T(4,128)(2,1)S(1)} all-reduce(bf16[2,3,3,256]{3,1,2,0:T(4,128)(2,1)S(1)} %copy.225), channel_id=1, replica_groups=mesh['seq'=16,'wr'=4,'wc'=4] {'seq'}, use_global_device_ids=true, to_apply=%region_38.39 | all-reduce | flops 4608 | bytes 18432 | tf_op jit(solution)/shard_map/psum | solution.py:253
  618.3 4.1 copy.283
  624.0 2.8 copy.282
  626.8 2.6 fusion.10
  (283 shorter events, 79.6 us)
Async XLA Ops:
  7.2 56.5 %all-gather.9.cloned.1.call-start = ((), (), s32[]{:S(2)}) async-start(), calls=%async_computation.8 | async-start | bytes 2228224 | tf_op jit(solution)/shard_map/all_gather | solution.py:153
  7.9 108.9 %all-gather.11.cloned.1.call-start = ((), (), s32[]{:S(2)}) async-start(), calls=%async_computation.9 | async-start | bytes 1310720 | tf_op jit(solution)/shard_map/all_gather | solution.py:170
  12.7 7.3 %copy-start.36 = (s32[512]{0:T(512)}, s32[512]{0:T(512)S(1)}, u32[]{:S(2)}) copy-start(s32[512]{0:T(512)S(1)} %convert_add_fusion) | copy-start | bytes 6148
  15.8 57.2 %copy-start.52 = (f32[4]{0:T(128)}, f32[4]{0:T(128)S(1)}, u32[]{:S(2)}) copy-start(f32[4]{0:T(128)S(1)} %compare_convert_fusion.6) | copy-start | bytes 52
  20.1 54.4 %copy-start.24 = (f32[512]{0:T(512)}, f32[512]{0:T(512)S(1)}, u32[]{:S(2)}) copy-start(f32[512]{0:T(512)S(1)} %get-tuple-element.95) | copy-start | bytes 6148
  20.1 54.4 %copy-start.26 = (f32[512]{0:T(512)}, f32[512]{0:T(512)S(1)}, u32[]{:S(2)}) copy-start(f32[512]{0:T(512)S(1)} %get-tuple-element.96) | copy-start | bytes 6148
  20.1 54.4 %copy-start.28 = (f32[512]{0:T(512)}, f32[512]{0:T(512)S(1)}, u32[]{:S(2)}) copy-start(f32[512]{0:T(512)S(1)} %get-tuple-element.97) | copy-start | bytes 6148
  69.2 5.2 copy-start.7
  70.6 3.8 collective-permute-start
  74.9 11.2 %copy-start.18 = (bf16[512,256]{1,0:T(8,128)(2,1)}, bf16[512,256]{1,0:T(8,128)(2,1)S(1)}, u32[]{:S(2)}) copy-start(bf16[512,256]{1,0:T(8,128)(2,1)S(1)} %multiply_convert_fusion.5) | copy-start | bytes 786436
  76.1 25.0 %all-to-all-start = ((bf16[4,512,256]{1,2,0:T(8,128)(2,1)}), bf16[4,512,256]{1,2,0:T(8,128)(2,1)S(1)}, u32[]{:S(2)}, u32[]{:S(2)}) async-start(bf16[4,512,256]{1,2,0:T(8,128)(2,1)} %stack.66), calls=%async_computation | async-start | bytes 2097152 | tf_op jit(solution)/shard_map/all_to_all | solution.py:172
  81.5 25.1 %copy-start.34 = (f32[512]{0:T(512)}, f32[512]{0:T(512)S(1)}, u32[]{:S(2)}) copy-start(f32[512]{0:T(512)S(1)} %get-tuple-element.59) | copy-start | bytes 6148
  101.1 5.4 copy-start.11
  125.4 8.6 %copy-start.23 = (f32[2,1,4,4,256]{4,3,2,1,0:T(4,128)S(1)}, f32[2,1,4,4,256]{4,3,2,1,0:T(4,128)}, u32[]{:S(2)}) copy-start(f32[2,1,4,4,256]{4,3,2,1,0:T(4,128)} %param.24) | copy-start | bytes 98308
  125.4 10.2 %copy-start.68 = (u32[256]{0:T(256)S(1)}, u32[256]{0:T(256)}, u32[]{:S(2)}) copy-start(u32[256]{0:T(256)} %constant.135) | copy-start | bytes 3076
  125.4 72.2 %all-to-all-start.1 = ((bf16[16,3,64,256]{3,2,1,0:T(8,128)(2,1)}), bf16[16,3,64,256]{3,2,1,0:T(8,128)(2,1)}, u32[]{:S(2)}, u32[]{:S(2)}) async-start(bf16[16,3,64,256]{3,2,1,0:T(8,128)(2,1)} %pad_maximum_fusion.6), calls=%async_computation.1 | async-start | bytes 3145728 | tf_op jit(solution)/shard_map/all_to_all | solution.py:211
  137.5 59.9 %copy-start.48 = (s32[17]{0:T(128)}, s32[17]{0:T(128)S(1)}, u32[]{:S(2)}) copy-start(s32[17]{0:T(128)S(1)} %fusion.174) | copy-start | bytes 208
  138.2 59.2 %copy-start.50 = (s32[16]{0:T(128)}, s32[16]{0:T(128)S(1)}, u32[]{:S(2)}) copy-start(s32[16]{0:T(128)S(1)} %fusion.173) | copy-start | bytes 196
  138.3 59.0 %copy-start.30 = (pred[17,16]{0,1:T(8,128)(4,1)}, pred[17,16]{0,1:T(8,128)(4,1)S(1)}, u32[]{:S(2)}) copy-start(pred[17,16]{0,1:T(8,128)(4,1)S(1)} %iota_compare_fusion.2) | copy-start | bytes 820
  138.3 59.0 %copy-start.31 = (pred[16,16]{1,0:T(8,128)(4,1)}, pred[16,16]{1,0:T(8,128)(4,1)S(1)}, u32[]{:S(2)}) copy-start(pred[16,16]{1,0:T(8,128)(4,1)S(1)} %iota_compare_fusion.1) | copy-start | bytes 772
  199.3 11.2 %copy-start.57 = (f32[2,256]{1,0:T(2,128)S(1)}, f32[2,256]{1,0:T(2,128)}, u32[]{:S(2)}) copy-start(f32[2,256]{1,0:T(2,128)} %param.27) | copy-start | bytes 6148
  199.4 11.8 %copy-start.58 = (f32[2,256]{1,0:T(2,128)S(1)}, f32[2,256]{1,0:T(2,128)}, u32[]{:S(2)}) copy-start(f32[2,256]{1,0:T(2,128)} %param.28) | copy-start | bytes 6148
  203.6 20.4 %all-to-all-start.2 = ((bf16[16,64,256]{2,1,0:T(8,128)(2,1)}), bf16[16,64,256]{2,1,0:T(8,128)(2,1)}, u32[]{:S(2)}, u32[]{:S(2)}) async-start(bf16[16,64,256]{2,1,0:T(8,128)(2,1)} %multiply_reduce_fusion.1), calls=%async_computation.2 | async-start | bytes 1048576 | tf_op jit(solution)/shard_map/all_to_all | solution.py:214
  210.5 112.2 %all-gather.13.cloned.1.call-start = ((), (), s32[]{:S(2)}) async-start(), calls=%async_computation.10 | async-start | bytes 2228224 | tf_op jit(solution)/shard_map/all_gather | solution.py:153
  211.7 5.7 copy-start.35
  211.7 5.7 copy-start.37
  211.7 5.7 copy-start.47
  217.4 6.5 %copy-start.60 = (f32[512]{0:T(512)S(1)}, f32[512]{0:T(512)}, u32[]{:S(2)}) copy-start(f32[512]{0:T(512)} %get-tuple-element.57) | copy-start | bytes 6148
  276.0 107.6 %all-gather.15.cloned.1.call-start = ((), (), s32[]{:S(2)}) async-start(), calls=%async_computation.11 | async-start | bytes 1310720 | tf_op jit(solution)/shard_map/all_gather | solution.py:170
  328.2 4.7 copy-start.59
  328.2 7.0 %copy-start.25 = (f32[512]{0:T(512)S(1)}, f32[512]{0:T(512)}, u32[]{:S(2)}) copy-start(f32[512]{0:T(512)} %copy-done.24) | copy-start | bytes 6148
  328.3 7.0 %copy-start.27 = (f32[512]{0:T(512)S(1)}, f32[512]{0:T(512)}, u32[]{:S(2)}) copy-start(f32[512]{0:T(512)} %copy-done.26) | copy-start | bytes 6148
  328.3 7.0 %copy-start.29 = (f32[512]{0:T(512)S(1)}, f32[512]{0:T(512)}, u32[]{:S(2)}) copy-start(f32[512]{0:T(512)} %copy-done.28) | copy-start | bytes 6148
  328.3 7.0 %copy-start.39 = (f32[1,1,256]{2,1,0:T(1,128)S(1)}, f32[1,1,256]{2,1,0:T(1,128)}, u32[]{:S(2)}) copy-start(f32[1,1,256]{2,1,0:T(1,128)} %get-tuple-element.80) | copy-start | bytes 3076
  328.3 7.0 %copy-start.40 = (f32[1,1,256]{2,1,0:T(1,128)S(1)}, f32[1,1,256]{2,1,0:T(1,128)}, u32[]{:S(2)}) copy-start(f32[1,1,256]{2,1,0:T(1,128)} %get-tuple-element.81) | copy-start | bytes 3076
  328.3 7.0 %copy-start.41 = (f32[1,1,256]{2,1,0:T(1,128)S(1)}, f32[1,1,256]{2,1,0:T(1,128)}, u32[]{:S(2)}) copy-start(f32[1,1,256]{2,1,0:T(1,128)} %get-tuple-element.86) | copy-start | bytes 3076
  328.3 7.0 %copy-start.42 = (f32[1,1,256]{2,1,0:T(1,128)S(1)}, f32[1,1,256]{2,1,0:T(1,128)}, u32[]{:S(2)}) copy-start(f32[1,1,256]{2,1,0:T(1,128)} %get-tuple-element.87) | copy-start | bytes 3076
  328.3 7.0 %copy-start.43 = (f32[1,256]{1,0:T(1,128)S(1)}, f32[1,256]{1,0:T(1,128)}, u32[]{:S(2)}) copy-start(f32[1,256]{1,0:T(1,128)} %get-tuple-element.108) | copy-start | bytes 3076
  330.5 3.8 collective-permute-start.1
  336.4 8.7 %copy-start.44 = (pred[512]{0:T(512)(128)(4,1)S(1)}, pred[512]{0:T(512)(128)(4,1)}, u32[]{:S(2)}) copy-start(pred[512]{0:T(512)(128)(4,1)} %get-tuple-element.58) | copy-start | bytes 1540
  336.4 10.0 %copy-start.54 = (pred[512]{0:T(512)(128)(4,1)S(1)}, pred[512]{0:T(512)(128)(4,1)}, u32[]{:S(2)}) copy-start(pred[512]{0:T(512)(128)(4,1)} %get-tuple-element.65) | copy-start | bytes 1540
  336.4 10.0 %copy-start.55 = (pred[512]{0:T(512)(128)(4,1)S(1)}, pred[512]{0:T(512)(128)(4,1)}, u32[]{:S(2)}) copy-start(pred[512]{0:T(512)(128)(4,1)} %get-tuple-element.92) | copy-start | bytes 1540
  336.4 10.0 %copy-start.56 = (pred[512]{0:T(512)(128)(4,1)S(1)}, pred[512]{0:T(512)(128)(4,1)}, u32[]{:S(2)}) copy-start(pred[512]{0:T(512)(128)(4,1)} %get-tuple-element.94) | copy-start | bytes 1540
  340.3 22.6 %all-to-all-start.4 = ((bf16[4,512,256]{1,2,0:T(8,128)(2,1)}), bf16[4,512,256]{1,2,0:T(8,128)(2,1)}, u32[]{:S(2)}, u32[]{:S(2)}) async-start(bf16[4,512,256]{1,2,0:T(8,128)(2,1)} %stack.69), calls=%async_computation.4 | async-start | bytes 2097152 | tf_op jit(solution)/shard_map/all_to_all | solution.py:172
  345.8 24.9 %copy-start.32 = (f32[512]{0:T(512)}, f32[512]{0:T(512)S(1)}, u32[]{:S(2)}) copy-start(f32[512]{0:T(512)S(1)} %get-tuple-element.54) | copy-start | bytes 6148
  396.9 11.4 %copy-start.64 = (f32[16]{0:T(128)S(1)}, f32[16]{0:T(128)}, u32[]{:S(2)}) copy-start(f32[16]{0:T(128)} %get-tuple-element.34) | copy-start | bytes 196
  396.9 12.0 %copy-start.63 = (f32[16]{0:T(128)S(1)}, f32[16]{0:T(128)}, u32[]{:S(2)}) copy-start(f32[16]{0:T(128)} %get-tuple-element.33) | copy-start | bytes 196
  396.9 81.8 %all-to-all-start.5 = ((bf16[16,3,64,256]{3,2,1,0:T(8,128)(2,1)}), bf16[16,3,64,256]{3,2,1,0:T(8,128)(2,1)}, u32[]{:S(2)}, u32[]{:S(2)}) async-start(bf16[16,3,64,256]{3,2,1,0:T(8,128)(2,1)} %pad_maximum_fusion.7), calls=%async_computation.5 | async-start | bytes 3145728 | tf_op jit(solution)/shard_map/all_to_all | solution.py:211
  405.8 212.6 %all-gather.17.cloned.1.call-start = ((), (), s32[]{:S(2)}) async-start(), calls=%async_computation.12 | async-start | bytes 1671168 | tf_op jit(solution)/shard_map/all_gather | solution.py:219
  409.7 66.8 %copy-start.49 = (s32[17]{0:T(128)S(1)}, s32[17]{0:T(128)}, u32[]{:S(2)}) copy-start(s32[17]{0:T(128)} %copy-done.48) | copy-start | bytes 208
  409.7 66.8 %copy-start.51 = (s32[16]{0:T(128)S(1)}, s32[16]{0:T(128)}, u32[]{:S(2)}) copy-start(s32[16]{0:T(128)} %copy-done.50) | copy-start | bytes 196
  484.8 22.6 %all-to-all-start.6 = ((bf16[16,64,256]{2,1,0:T(8,128)(2,1)}), bf16[16,64,256]{2,1,0:T(8,128)(2,1)}, u32[]{:S(2)}, u32[]{:S(2)}) async-start(bf16[16,64,256]{2,1,0:T(8,128)(2,1)} %multiply_reduce_fusion), calls=%async_computation.6 | async-start | bytes 1048576 | tf_op jit(solution)/shard_map/all_to_all | solution.py:214
  491.5 5.8 copy-start.33
  491.6 5.8 copy-start.38
  491.6 5.8 copy-start.46
  491.6 132.4 %all-gather.19.cloned.1.call-start = ((), (), s32[]{:S(2)}) async-start(), calls=%async_computation.13 | async-start | bytes 1671168 | tf_op jit(solution)/shard_map/all_gather | solution.py:219
  501.0 6.5 %copy-start.45 = (f32[512]{0:T(512)S(1)}, f32[512]{0:T(512)}, u32[]{:S(2)}) copy-start(f32[512]{0:T(512)} %get-tuple-element.53) | copy-start | bytes 6148
  502.7 14.6 %copy-start.3 = (bf16[512,2048]{1,0:T(8,128)(2,1)S(1)}, bf16[512,2048]{1,0:T(8,128)(2,1)}, u32[]{:S(2)}) copy-start(bf16[512,2048]{1,0:T(8,128)(2,1)} %copy-done.2) | copy-start | bytes 6291460
  502.7 14.6 %copy-start.17 = (bf16[512,256]{1,0:T(8,128)(2,1)S(1)}, bf16[512,256]{1,0:T(8,128)(2,1)}, u32[]{:S(2)}) copy-start(bf16[512,256]{1,0:T(8,128)(2,1)} %multiply_convert_fusion.3) | copy-start | bytes 786436
  502.7 14.6 %copy-start.61 = (f32[1,256]{1,0:T(1,128)S(1)}, f32[1,256]{1,0:T(1,128)}, u32[]{:S(2)}) copy-start(f32[1,256]{1,0:T(1,128)} %get-tuple-element.102) | copy-start | bytes 3076
  502.7 14.6 %copy-start.62 = (f32[1,256]{1,0:T(1,128)S(1)}, f32[1,256]{1,0:T(1,128)}, u32[]{:S(2)}) copy-start(f32[1,256]{1,0:T(1,128)} %get-tuple-element.100) | copy-start | bytes 3076
  526.0 7.7 %copy-start.8 = (bf16[512,256]{1,0:T(8,128)(2,1)S(1)}, bf16[512,256]{1,0:T(8,128)(2,1)}, u32[]{:S(2)}) copy-start(bf16[512,256]{1,0:T(8,128)(2,1)} %convolution_convert_fusion.10) | copy-start | bytes 786436
  526.0 91.6 %copy-start.67 = (s32[2]{0:T(128)S(1)}, s32[2]{0:T(128)}, u32[]{:S(2)}) copy-start(s32[2]{0:T(128)} %param.31) | copy-start | bytes 28
  526.0 96.4 %all-to-all-start.7 = ((bf16[512,16,128]{2,0,1:T(8,128)(2,1)}), bf16[512,16,128]{2,0,1:T(8,128)(2,1)S(1)}, u32[]{:S(2)}, u32[]{:S(2)}) async-start(bf16[512,16,128]{2,0,1:T(8,128)(2,1)} %bitcast.283), calls=%async_computation.7 | async-start | bytes 4194304 | tf_op jit(solution)/shard_map/all_to_all | solution.py:237
  (20 other events, 42.3 us)
Sparse Core Ops, SparseCore 0:
  10.6 53.0 all-gather.8
  69.3 28.9 all-gather.10
  276.1 46.5 all-gather.12
  329.9 25.5 all-gather.14
  474.9 71.9 all-gather.16
  548.5 70.0 all-gather.18
